TPU v7x, 32 devices: a whole 2x2x4 slice. The times are simulated.
32 devices in a mesh: row: 8 (over z, x), col: 4 (over y, core).
Axes of the slice: x: 2, y: 2, z: 4, core: 2. Of those that a mesh axis runs over, the one named last changes fastest.
Arguments:
- diagonal_inverses: bfloat16 [24, 2048, 2048], P('row', 'col'), may hold values from -0.125 to 0.125
- column_basis: bfloat16 [24, 2048, 256], P('row', 'col'), may hold values from -6 to 6
- row_basis: bfloat16 [24, 2048, 256], P('row', 'col'), may hold values from -0.125 to 0.125
- transfer: float32 [24, 256, 256], P('row', 'col'), may hold values from -0.375 to 0.375
- coupling: float32 [24, 256, 256], P('row', 'col'), may hold values from -6 to 6
- ranks: int32 [24], P('row'), may hold values from 128 to 256, as said below
Outputs:
- merged: float32 [24, 256, 256], P('row', 'col')
- parent_skeleton: float32 [24, 256, 256], P('row', 'col')
Inputs may be any that keep to these rules, and one draw needn't show every extreme that they name: `ranks`: each rank is 128 or 256; both occur in every draw.
All inputs are finite; a program needn't handle non-finite values.
Results may differ from a plain program's by a relative error of at most 0.0021.
Values may be sent and summed in bfloat16 or wider, within the bound.
A program may use at most 64 MiB of HBM per device.

v0:
```python
import jax
import jax.numpy as jnp
from jax import lax
from jax.sharding import PartitionSpec as P

BIT = 2


def swapped(block, axis, bit):
    count = lax.axis_size(axis)
    route = []
    for low in range(count):
        high = low | 1 << bit
        if high != low and high < count:
            route += [(low, high), (high, low)]
    return lax.ppermute(block, axis, route)


def shards(diagonal_inverses, column_basis, row_basis, transfer, coupling, ranks):
    rank_width = transfer.shape[2]
    part_rows = transfer.shape[1]
    highest = lax.Precision.HIGHEST
    live_cols = jnp.arange(rank_width, dtype=jnp.int32)[None, :] < ranks[:, None]
    left_factor_basis = jnp.where(live_cols[:, None, :], column_basis, jnp.zeros_like(column_basis))
    right_factor_basis = jnp.where(live_cols[:, None, :], row_basis, jnp.zeros_like(row_basis))
    eliminated_part = jnp.einsum(
        "nmp,npr->nmr",
        diagonal_inverses,
        lax.all_gather(left_factor_basis, "col", axis=1, tiled=True),
        preferred_element_type=jnp.float32,
    ).astype(jnp.bfloat16)
    skeleton = jnp.transpose(
        lax.psum_scatter(
            jnp.einsum(
                "hgp,hgd->phd",
                right_factor_basis,
                eliminated_part,
                preferred_element_type=jnp.float32,
            ),
            "col",
            scatter_dimension=0,
            tiled=True,
        ),
        (1, 0, 2),
    )
    offset_rows = lax.axis_index("col") * part_rows
    active_rows = lax.dynamic_slice_in_dim(live_cols, offset_rows, part_rows, 1)
    masked = transfer * active_rows[:, :, None].astype(jnp.float32)
    masked_sib = swapped(masked, "row", BIT)
    complete_local_block, whole_sib = (
        lax.all_gather(masked, "col", axis=1, tiled=True),
        lax.all_gather(masked_sib, "col", axis=1, tiled=True),
    )
    merged = jnp.einsum("nij,njk->nik", skeleton, complete_local_block, precision=highest)
    merged = merged + jnp.einsum("nij,njk->nik", coupling, whole_sib, precision=highest)
    own_term = jnp.transpose(
        lax.psum_scatter(
            jnp.einsum("nji,njk->ink", masked, merged, precision=highest),
            "col",
            scatter_dimension=0,
            tiled=True,
        ),
        (1, 0, 2),
    )
    parent = own_term + swapped(own_term, "row", BIT)
    return (merged, parent)


def solution(mesh):
    placed = (
        P("row", "col", None),
        P("row", "col", None),
        P("row", "col", None),
        P("row", "col", None),
        P("row", "col", None),
        P("row"),
    )
    return jax.shard_map(
        shards,
        mesh=mesh,
        in_specs=placed,
        out_specs=(P("row", "col", None), P("row", "col", None)),
        check_vma=False,
    )
```

profile of v0, /device:TPU:0, one launch (start us, length us, event | category | flops | bytes accessed | tf_op | source)
XLA Modules:
  0.0 138.4 jit_solution(1713739336658735654)
XLA Ops:
  7.2 0.0 copy-start
  7.2 0.0 all-gather.2.cloned.1.call-start
  7.2 0.8 iota_compare_fusion
  8.0 2.1 %broadcast_select_fusion = bf16[3,512,256]{2,1,0:T(8,128)(2,1)} fusion(bf16[3,512,256]{2,1,0:T(8,128)(2,1)} %param.7, pred[3,256]{1,0:T(4,128)(4,1)S(1)} %iota_compare_fusion), kind=kLoop, calls=%fused_computation.7 | loop fusion | flops 393216 | bytes 1573632 | tf_op jit(solution)/shard_map/jit(_where)/select_n | solution.py:24
  10.1 0.0 all-gather.2.cloned.1.call-update
  10.1 0.0 copy-start.2
  10.1 0.0 reduce-scatter.2.cloned.1.call-start
  10.2 31.3 %all-gather.2.cloned.1.call-done = bf16[3,2048,256]{2,1,0:T(8,128)(2,1)} async-done(((bf16[3,512,256]{2,1,0:T(8,128)(2,1)}), bf16[3,2048,256]{2,1,0:T(8,128)(2,1)}) %all-gather.2.cloned.1.call-update) | async-done | bytes 3145744 | tf_op jit(solution)/shard_map/all_gather | solution.py:29
  41.5 7.1 %convolution_bitcast_fusion = f32[256,3,256]{2,0,1:T(8,128)} fusion(bf16[3,2048,256]{2,1,0:T(8,128)(2,1)} %all-gather.2.cloned.1.call-done, bf16[3,512,2048]{2,1,0:T(8,128)(2,1)} %param.6, bf16[3,512,256]{2,1,0:T(8,128)(2,1)} %param.8, pred[3,256]{1,0:T(4,128)(4,1)S(1)} %iota_compare_fusion), kind=kOutput, calls=%fused_computation.1 | convolution fusion | flops 1812725760 | bytes 11010816 | tf_op jit(solution)/shard_map/hgp,hgd->phd/dot_general | solution.py:34
  48.6 0.0 reduce-scatter.2.cloned.1.call-update
  48.6 0.0 all-reduce.3.cloned.1.call-start
  48.7 0.1 dynamic-slice_convert_fusion
  48.8 0.0 copy-done.2
  48.8 0.1 broadcast_multiply_fusion
  48.9 2.5 %collective-permute-start = (f32[3,64,256]{2,1,0:T(8,128)S(1)}, f32[3,64,256]{2,1,0:T(8,128)S(1)}, u32[]{:S(2)}, u32[]{:S(2)}) collective-permute-start(f32[3,64,256]{2,1,0:T(8,128)S(1)} %broadcast_multiply_fusion), channel_id=1, source_target_pairs={{0,16},{16,0},{4,20},{20,4},{8,24},{24,8},{12,28},{28,12},{1,17},{... | collective-permute-start | bytes 589832 | tf_op jit(solution)/shard_map/ppermute | solution.py:16
  51.3 8.3 %all_gather.10 = f32[3,256,256]{2,1,0:T(8,128)S(1)} all-gather(f32[3,64,256]{2,1,0:T(8,128)S(1)} %broadcast_multiply_fusion), channel_id=1, replica_groups=mesh['row'=8,'col'=4] {'col'}, dimensions={1}, use_global_device_ids=true | all-gather | bytes 983040 | tf_op jit(solution)/shard_map/all_gather | solution.py:51
  59.6 1.4 %collective-permute-done = f32[3,64,256]{2,1,0:T(8,128)S(1)} collective-permute-done((f32[3,64,256]{2,1,0:T(8,128)S(1)}, f32[3,64,256]{2,1,0:T(8,128)S(1)}, u32[]{:S(2)}, u32[]{:S(2)}) %collective-permute-start) | collective-permute-done | bytes 196640 | tf_op jit(solution)/shard_map/ppermute | solution.py:16
  61.1 10.0 %all_gather.11 = f32[3,256,256]{2,1,0:T(8,128)S(1)} all-gather(f32[3,64,256]{2,1,0:T(8,128)S(1)} %collective-permute-done), channel_id=1, replica_groups=mesh['row'=8,'col'=4] {'col'}, dimensions={1}, use_global_device_ids=true | all-gather | bytes 983040 | tf_op jit(solution)/shard_map/all_gather | solution.py:52
  71.1 0.0 copy-start.3
  71.1 2.1 %reduce-scatter.2.cloned.1.call-done = f32[64,3,256]{2,0,1:T(8,128)} async-done(((f32[256,3,256]{2,0,1:T(8,128)}), f32[64,3,256]{2,0,1:T(8,128)}) %reduce-scatter.2.cloned.1.call-update) | async-done | bytes 196624 | tf_op jit(solution)/shard_map/reduce_scatter | solution.py:33
  73.2 1.5 %fusion.4 = f32[3,64,256]{2,1,0:T(8,128)S(1)} fusion(f32[3,256,256]{2,1,0:T(8,128)S(1)} %all_gather.10, f32[64,3,256]{2,0,1:T(8,128)} %reduce-scatter.2.cloned.1.call-done), kind=kOutput, calls=%fused_computation.10 | convolution fusion | flops 150994944 | bytes 1179648 | tf_op jit(solution)/shard_map/nij,njk->nik/dot_general | solution.py:54
  74.7 0.0 copy-done
  74.7 0.6 fusion
  75.4 0.0 copy-start.1
  75.4 0.8 convolution_bitcast_fusion.1
  76.2 1.4 copy.9
  77.6 0.0 all-reduce.3.cloned.1.call-update
  77.6 0.0 copy-done.3
  77.6 0.6 dynamic-slice
  78.8 36.0 %all-reduce.3.cloned.1.call-done = f32[256,3,256]{2,1,0:T(4,128)} async-done(((f32[256,3,256]{2,1,0:T(4,128)}), f32[256,3,256]{2,1,0:T(4,128)}) %all-reduce.3.cloned.1.call-update) | async-done | bytes 786448
  114.8 1.0 dynamic-slice_bitcast_fusion
  115.8 2.5 %collective-permute-start.1 = (f32[3,64,256]{2,0,1:T(4,128)S(1)}, f32[3,64,256]{2,0,1:T(4,128)S(1)}, u32[]{:S(2)}, u32[]{:S(2)}) collective-permute-start(f32[3,64,256]{2,0,1:T(4,128)S(1)} %dynamic-slice_bitcast_fusion), channel_id=1, source_target_pairs={{0,16},{16,0},{4,20},{20,4},{8,24},{24,8},{12,28},{28,12},{1,17},{... | collective-permute-start | bytes 589832 | tf_op jit(solution)/shard_map/ppermute | solution.py:16
  118.3 11.8 %collective-permute-done.1 = f32[3,64,256]{2,0,1:T(4,128)S(1)} collective-permute-done((f32[3,64,256]{2,0,1:T(4,128)S(1)}, f32[3,64,256]{2,0,1:T(4,128)S(1)}, u32[]{:S(2)}, u32[]{:S(2)}) %collective-permute-start.1) | collective-permute-done | bytes 196640 | tf_op jit(solution)/shard_map/ppermute | solution.py:16
  130.1 1.0 fusion.14
  131.1 0.7 copy.10
  131.9 0.0 copy-done.1
Async XLA Ops:
  7.2 67.6 %copy-start = (f32[3,64,256]{2,1,0:T(8,128)S(1)}, f32[3,64,256]{2,1,0:T(8,128)}, u32[]{:S(2)}) copy-start(f32[3,64,256]{2,1,0:T(8,128)} %param.10) | copy-start | bytes 589828
  7.2 34.3 %all-gather.2.cloned.1.call-start = ((), (), s32[]{:S(2)}) async-start(), calls=%async_computation.1 | async-start | bytes 3932160 | tf_op jit(solution)/shard_map/all_gather | solution.py:29
  10.1 38.7 %copy-start.2 = (f32[3,64,256]{2,1,0:T(8,128)S(1)}, f32[3,64,256]{2,1,0:T(8,128)}, u32[]{:S(2)}) copy-start(f32[3,64,256]{2,1,0:T(8,128)} %param.9) | copy-start | bytes 589828
  10.1 63.1 %reduce-scatter.2.cloned.1.call-start = ((), (), s32[]{:S(2)}) async-start(), calls=%async_computation.2 | async-start | bytes 983040 | tf_op jit(solution)/shard_map/reduce_scatter | solution.py:33
  48.6 66.2 %all-reduce.3.cloned.1.call-start = ((), (), s32[]{:S(2)}) async-start(), calls=%async_computation.3 | async-start | bytes 2097152
  48.9 12.2 %collective-permute-start = (f32[3,64,256]{2,1,0:T(8,128)S(1)}, f32[3,64,256]{2,1,0:T(8,128)S(1)}, u32[]{:S(2)}, u32[]{:S(2)}) collective-permute-start(f32[3,64,256]{2,1,0:T(8,128)S(1)} %broadcast_multiply_fusion), channel_id=1, source_target_pairs={{0,16},{16,0},{4,20},{20,4},{8,24},{24,8},{12,28},{28,12},{1,17},{... | collective-permute-start | bytes 589832 | tf_op jit(solution)/shard_map/ppermute | solution.py:16
  71.1 6.5 %copy-start.3 = (u32[32]{0:T(128)S(1)}, u32[32]{0:T(128)}, u32[]{:S(2)}) copy-start(u32[32]{0:T(128)} %constant.20) | copy-start | bytes 388
  75.4 56.5 %copy-start.1 = (f32[3,64,256]{2,1,0:T(8,128)}, f32[3,64,256]{2,1,0:T(8,128)S(1)}, u32[]{:S(2)}) copy-start(f32[3,64,256]{2,1,0:T(8,128)S(1)} %fusion) | copy-start | bytes 589828
  115.8 14.3 %collective-permute-start.1 = (f32[3,64,256]{2,0,1:T(4,128)S(1)}, f32[3,64,256]{2,0,1:T(4,128)S(1)}, u32[]{:S(2)}, u32[]{:S(2)}) collective-permute-start(f32[3,64,256]{2,0,1:T(4,128)S(1)} %dynamic-slice_bitcast_fusion), channel_id=1, source_target_pairs={{0,16},{16,0},{4,20},{20,4},{8,24},{24,8},{12,28},{28,12},{1,17},{... | collective-permute-start | bytes 589832 | tf_op jit(solution)/shard_map/ppermute | solution.py:16
Sparse Core Ops, SparseCore 0:
  10.2 31.2 all-gather.1
  48.7 24.3 reduce-scatter.1
  77.7 37.0 all-reduce.2
where the time goes:
time: 139 us; the launch traced here: 138 us
  waiting for transfers between devices  82.7 us (59%)
  blocking collectives  18.3 us (13%)
  between operations  14.5 us (10%)
  matrix products  10.1 us (7%)
  starting transfers between devices  5.07 us (4%)
  other arithmetic  4.03 us (3%)
  local copies, waits for them, and re-layouts  3.68 us (3%)
    unnamed x4, waiting for transfers between devices  36 us
    all_gather x1, waiting for transfers between devices, shards(): lax.all_gather(left_factor_basis, 'col', axis=1, tiled=True)  31.3 us
    ppermute x2, waiting for transfers between devices, swapped(): return lax.ppermute(block, axis, route)  13.3 us
    all_gather x1, blocking collectives, shards(): lax.all_gather(masked_sib, 'col', axis=1, tiled=True)  9.98 us
    all_gather x1, blocking collectives, shards(): lax.all_gather(masked, 'col', axis=1, tiled=True)  8.3 us
    dot_general x1, matrix products, shards(): jnp.einsum('hgp,hgd->phd', right_factor_basis, eliminated_part, preferred...  7.12 us
    ppermute x2, starting transfers between devices, swapped(): return lax.ppermute(block, axis, route)  4.94 us
  transfers between devices with their start and end apart: 5, of which 5 were waited for; matrix products, arithmetic and copies ran while one was open for 1% of the time, Pallas kernels for 0%

commit v1 on v0

--- a/solution.py
+++ b/solution.py
@@ -4,6 +4,14 @@
 from jax.sharding import PartitionSpec as P
 
 BIT = 2
+
+
+def gather_from_all(shard, axis, dim):
+    size = lax.axis_size(axis)
+    repeats = [size if d == dim else 1 for d in range(shard.ndim)]
+    return lax.all_to_all(
+        jnp.tile(shard, repeats), axis, split_axis=dim, concat_axis=dim, tiled=True
+    )
 
 
 def swapped(block, axis, bit):
@@ -26,7 +34,7 @@
     eliminated_part = jnp.einsum(
         "nmp,npr->nmr",
         diagonal_inverses,
-        lax.all_gather(left_factor_basis, "col", axis=1, tiled=True),
+        gather_from_all(left_factor_basis, "col", 1),
         preferred_element_type=jnp.float32,
     ).astype(jnp.bfloat16)
     skeleton = jnp.transpose(

time: 139 us -> 161 us (1.16)
  blocking collectives: 18.3 us -> 68.3 us
  waiting for transfers between devices: 82.7 us -> 53.1 us
  local copies, waits for them, and re-layouts: 3.68 us -> 5.45 us
    all_to_all x0 -> x1, blocking collectives: none -> 52.4 us  [gather_from_all(): lax.all_to_all(jnp.tile(shard, repeats), axis, split_axis=dim, concat_axi...]
    all_gather x1 -> x0, waiting for transfers between devices: 31.3 us -> none  [shards(): lax.all_gather(left_factor_basis, 'col', axis=1, tiled=True)]
    reduce_scatter x1, waiting for transfers between devices: 2.13 us -> 3.96 us  [shards(): lax.psum_scatter(jnp.einsum('hgp,hgd->phd', right_factor_basis, eliminate...]
    all_gather x1, blocking collectives: 9.98 us -> 8.32 us  [shards(): lax.all_gather(masked_sib, 'col', axis=1, tiled=True)]
    unnamed x4 -> x3, waiting for transfers between devices: 36 us -> 36.2 us
  transfers between devices with their start and end apart: 5 -> 4, of which waited for: 5 -> 4; matrix products, arithmetic and copies ran while one was open for 1% -> 0% of each run, Pallas kernels for 0% -> 0%
where the time goes in v1:
time: 161 us
  blocking collectives  68.3 us (42%)
  waiting for transfers between devices  53.1 us (33%)
  between operations  14.8 us (9%)
  matrix products  10.4 us (6%)
  starting transfers between devices  5.92 us (4%)
  local copies, waits for them, and re-layouts  5.45 us (3%)
  other arithmetic  3.15 us (2%)
    all_to_all x1, blocking collectives, gather_from_all(): lax.all_to_all(jnp.tile(shard, repeats), axis, split_axis=dim, concat_axi...  52.4 us
    unnamed x3, waiting for transfers between devices  36.2 us
    ppermute x2, waiting for transfers between devices, swapped(): return lax.ppermute(block, axis, route)  13 us
    all_gather x1, blocking collectives, shards(): lax.all_gather(masked_sib, 'col', axis=1, tiled=True)  8.32 us
    all_gather x1, blocking collectives, shards(): lax.all_gather(masked, 'col', axis=1, tiled=True)  7.53 us
    dot_general x1, matrix products, shards(): jnp.einsum('hgp,hgd->phd', right_factor_basis, eliminated_part, preferred...  7.38 us
    ppermute x2, starting transfers between devices, swapped(): return lax.ppermute(block, axis, route)  5.84 us
    reduce_scatter x1, waiting for transfers between devices, shards(): lax.psum_scatter(jnp.einsum('hgp,hgd->phd', right_factor_basis, eliminate...  3.96 us
  transfers between devices with their start and end apart: 4, of which 4 were waited for; matrix products, arithmetic and copies ran while one was open for 0% of the time, Pallas kernels for 0%

profile of v1, /device:TPU:0, one launch (start us, length us, event | category | flops | bytes accessed | tf_op | source)
XLA Modules:
  0.0 161.1 jit_solution(7371309907231867414)
XLA Ops:
  7.2 0.0 copy-start
  7.2 0.0 reduce-scatter.2.cloned.1.call-start
  7.2 0.8 iota_compare_fusion
  8.0 1.2 broadcast_select_fusion
  9.2 0.7 copy.9
  9.9 1.1 tile.4
  11.0 0.0 copy-start.3
  11.0 52.4 %all_to_all.5 = bf16[3,2048,256]{2,0,1:T(4,128)(2,1)} all-to-all(bf16[3,2048,256]{2,0,1:T(4,128)(2,1)S(1)} %bitcast.23), channel_id=1, replica_groups=mesh['row'=8,'col'=4] {'col'}, dimensions={1} | all-to-all | bytes 6291456 | tf_op jit(solution)/shard_map/all_to_all | solution.py:12
  63.4 0.0 copy-done.3
  63.4 0.0 copy-start.2
  63.4 7.4 %convolution_bitcast_fusion = f32[256,3,256]{2,0,1:T(8,128)} fusion(bf16[3,512,2048]{2,1,0:T(8,128)(2,1)} %param.6, bf16[3,2048,256]{2,0,1:T(4,128)(2,1)} %all_to_all.5, bf16[3,512,256]{2,1,0:T(8,128)(2,1)S(1)} %copy-done.3, pred[3,256]{1,0:T(4,128)(4,1)S(1)} %iota_compare_fusion), kind=kOutput, calls=%fused_computation.3 | convolution fusion | flops 1812725760 | bytes 11010816 | tf_op jit(solution)/shard_map/hgp,hgd->phd/dot_general | solution.py:42
  70.8 0.0 reduce-scatter.2.cloned.1.call-update
  70.8 0.0 all-reduce.3.cloned.1.call-start
  70.9 0.1 dynamic-slice_convert_fusion
  71.0 0.0 copy-done.2
  71.0 0.1 broadcast_multiply_fusion
  71.1 0.0 copy-start.4
  71.1 3.4 %collective-permute-start = (f32[3,64,256]{2,1,0:T(8,128)S(1)}, f32[3,64,256]{2,1,0:T(8,128)S(1)}, u32[]{:S(2)}, u32[]{:S(2)}) collective-permute-start(f32[3,64,256]{2,1,0:T(8,128)S(1)} %broadcast_multiply_fusion), channel_id=1, source_target_pairs={{0,16},{16,0},{4,20},{20,4},{8,24},{24,8},{12,28},{28,12},{1,17},{... | collective-permute-start | bytes 589832 | tf_op jit(solution)/shard_map/ppermute | solution.py:24
  74.4 7.5 %all_gather.6 = f32[3,256,256]{2,1,0:T(8,128)S(1)} all-gather(f32[3,64,256]{2,1,0:T(8,128)S(1)} %broadcast_multiply_fusion), channel_id=1, replica_groups=mesh['row'=8,'col'=4] {'col'}, dimensions={1}, use_global_device_ids=true | all-gather | bytes 983040 | tf_op jit(solution)/shard_map/all_gather | solution.py:59
  82.0 1.2 collective-permute-done
  83.2 8.3 %all_gather.7 = f32[3,256,256]{2,1,0:T(8,128)S(1)} all-gather(f32[3,64,256]{2,1,0:T(8,128)S(1)} %collective-permute-done), channel_id=1, replica_groups=mesh['row'=8,'col'=4] {'col'}, dimensions={1}, use_global_device_ids=true | all-gather | bytes 983040 | tf_op jit(solution)/shard_map/all_gather | solution.py:60
  91.5 4.0 %reduce-scatter.2.cloned.1.call-done = f32[64,3,256]{2,0,1:T(8,128)} async-done(((f32[256,3,256]{2,0,1:T(8,128)}), f32[64,3,256]{2,0,1:T(8,128)}) %reduce-scatter.2.cloned.1.call-update) | async-done | bytes 196624 | tf_op jit(solution)/shard_map/reduce_scatter | solution.py:41
  95.5 1.5 fusion.11
  97.0 0.0 copy-done
  97.0 0.6 fusion.7
  97.6 0.0 copy-start.1
  97.6 0.8 convolution_bitcast_fusion.1
  98.5 1.4 copy.10
  99.9 0.0 all-reduce.3.cloned.1.call-update
  99.9 0.0 copy-done.4
  99.9 0.6 dynamic-slice
  101.1 36.1 %all-reduce.3.cloned.1.call-done = f32[256,3,256]{2,1,0:T(4,128)} async-done(((f32[256,3,256]{2,1,0:T(4,128)}), f32[256,3,256]{2,1,0:T(4,128)}) %all-reduce.3.cloned.1.call-update) | async-done | bytes 786448
  137.3 1.0 dynamic-slice_bitcast_fusion
  138.3 2.5 %collective-permute-start.1 = (f32[3,64,256]{2,0,1:T(4,128)S(1)}, f32[3,64,256]{2,0,1:T(4,128)S(1)}, u32[]{:S(2)}, u32[]{:S(2)}) collective-permute-start(f32[3,64,256]{2,0,1:T(4,128)S(1)} %dynamic-slice_bitcast_fusion), channel_id=1, source_target_pairs={{0,16},{16,0},{4,20},{20,4},{8,24},{24,8},{12,28},{28,12},{1,17},{... | collective-permute-start | bytes 589832 | tf_op jit(solution)/shard_map/ppermute | solution.py:24
  140.7 11.8 %collective-permute-done.1 = f32[3,64,256]{2,0,1:T(4,128)S(1)} collective-permute-done((f32[3,64,256]{2,0,1:T(4,128)S(1)}, f32[3,64,256]{2,0,1:T(4,128)S(1)}, u32[]{:S(2)}, u32[]{:S(2)}) %collective-permute-start.1) | collective-permute-done | bytes 196640 | tf_op jit(solution)/shard_map/ppermute | solution.py:24
  152.5 1.0 fusion.20
  153.6 0.7 copy.11
  154.3 0.0 copy-done.1
Async XLA Ops:
  7.2 89.8 %copy-start = (f32[3,64,256]{2,1,0:T(8,128)S(1)}, f32[3,64,256]{2,1,0:T(8,128)}, u32[]{:S(2)}) copy-start(f32[3,64,256]{2,1,0:T(8,128)} %param.10) | copy-start | bytes 589828
  7.2 88.3 %reduce-scatter.2.cloned.1.call-start = ((), (), s32[]{:S(2)}) async-start(), calls=%async_computation.2 | async-start | bytes 983040 | tf_op jit(solution)/shard_map/reduce_scatter | solution.py:41
  11.0 52.5 %copy-start.3 = (bf16[3,512,256]{2,1,0:T(8,128)(2,1)S(1)}, bf16[3,512,256]{2,1,0:T(8,128)(2,1)}, u32[]{:S(2)}) copy-start(bf16[3,512,256]{2,1,0:T(8,128)(2,1)} %param.8) | copy-start | bytes 2359300
  63.4 7.5 %copy-start.2 = (f32[3,64,256]{2,1,0:T(8,128)S(1)}, f32[3,64,256]{2,1,0:T(8,128)}, u32[]{:S(2)}) copy-start(f32[3,64,256]{2,1,0:T(8,128)} %param.9) | copy-start | bytes 589828
  70.8 66.4 %all-reduce.3.cloned.1.call-start = ((), (), s32[]{:S(2)}) async-start(), calls=%async_computation.3 | async-start | bytes 2097152
  71.1 28.8 %copy-start.4 = (u32[32]{0:T(128)S(1)}, u32[32]{0:T(128)}, u32[]{:S(2)}) copy-start(u32[32]{0:T(128)} %constant.20) | copy-start | bytes 388
  71.1 12.1 %collective-permute-start = (f32[3,64,256]{2,1,0:T(8,128)S(1)}, f32[3,64,256]{2,1,0:T(8,128)S(1)}, u32[]{:S(2)}, u32[]{:S(2)}) collective-permute-start(f32[3,64,256]{2,1,0:T(8,128)S(1)} %broadcast_multiply_fusion), channel_id=1, source_target_pairs={{0,16},{16,0},{4,20},{20,4},{8,24},{24,8},{12,28},{28,12},{1,17},{... | collective-permute-start | bytes 589832 | tf_op jit(solution)/shard_map/ppermute | solution.py:24
  97.6 56.7 %copy-start.1 = (f32[3,64,256]{2,1,0:T(8,128)}, f32[3,64,256]{2,1,0:T(8,128)S(1)}, u32[]{:S(2)}) copy-start(f32[3,64,256]{2,1,0:T(8,128)S(1)} %fusion.7) | copy-start | bytes 589828
  138.3 14.3 %collective-permute-start.1 = (f32[3,64,256]{2,0,1:T(4,128)S(1)}, f32[3,64,256]{2,0,1:T(4,128)S(1)}, u32[]{:S(2)}, u32[]{:S(2)}) collective-permute-start(f32[3,64,256]{2,0,1:T(4,128)S(1)} %dynamic-slice_bitcast_fusion), channel_id=1, source_target_pairs={{0,16},{16,0},{4,20},{20,4},{8,24},{24,8},{12,28},{28,12},{1,17},{... | collective-permute-start | bytes 589832 | tf_op jit(solution)/shard_map/ppermute | solution.py:24
Sparse Core Ops, SparseCore 0:
  70.9 24.4 reduce-scatter.1
  100.0 37.2 all-reduce.2
